TPU v7x, 512 devices: a whole 4x8x8 slice. The times are simulated.
512 devices in a mesh: dp: 16 (over y, core), table: 32 (over x, z).
Axes of the slice: x: 4, y: 8, z: 8, core: 2. Of those that a mesh axis runs over, the one named last changes fastest.
Arguments:
- embedded: bfloat16 [2, 32768, 4096], P(None, 'dp', 'table'), may hold values from -1.1953125 to 1.1953125
- resid_grad: bfloat16 [2, 32768, 4096], P(None, 'dp', 'table'), may hold values from -0.29882812 to 0.29882812
- query_grad: bfloat16 [2, 32768, 2048], P(None, ('dp', 'table')), may hold values from -0.59765625 to 0.59765625
- query_weight: bfloat16 [4096, 2048], P('table'), may hold values from -0.09375 to 0.09375
- ngram_rows: int32 [2, 32768, 4], P(None, 'dp'), may hold values from 0 to 3199999, as said below
- touched_rows: int32 [32, 4, 12], replicated, may hold values from -1 to 3199999, as said below
- row_values: float32 [32, 4, 12, 1024], P('table'), may hold values from -6 to 6
- row_mean: float32 [32, 4, 12, 1024], P('table'), may hold values from -0.6 to 0.6
- row_square: float32 [32, 4, 12, 1024], P('table'), may hold values from 0.01 to 0.1
Outputs:
- weight_grad: float32 [4096, 2048], P('table')
- new_values: float32 [32, 4, 12, 1024], P('table')
- new_mean: float32 [32, 4, 12, 1024], P('table')
- new_square: float32 [32, 4, 12, 1024], P('table')
Inputs may be any that keep to these rules, and one draw needn't show every extreme that they name: `touched_rows`: owner o's list for slice s holds 1 to 12 distinct row ids of [o * 100000, (o + 1) * 100000) first, then -1; in every slice some owner's list is full. `ngram_rows`: every id of slice s is one of the listed rows of owner id // 100000 for slice s.
All inputs are finite; a program needn't handle non-finite values.
Results may differ from a plain program's by a relative error of at most 0.0003.
Values may be sent and summed in bfloat16 or wider, within the bound.
No kernel may reach another device: no remote copies, remote signals or barrier semaphores. Data moves between devices by JAX's collectives and lax.ppermute only.
A program may use at most 64 MiB of HBM per device.

v0:
```python
import jax
import jax.numpy as jnp
from jax import lax
from jax.sharding import PartitionSpec as P

SLICES = 4
SW = 1024
beta_one = 0.9
beta_two = 0.95
learn_rate = 0.01
adam_eps = 1e-08
adam_step = 10


def adam_rows(grads, values, mean, square, live):
    corr_one = 1.0 - beta_one**adam_step
    corr_two = 1.0 - beta_two**adam_step
    mean_next = beta_one * mean + (1.0 - beta_one) * grads
    square_next = beta_two * square + (1.0 - beta_two) * grads * grads
    update = learn_rate * (mean_next / corr_one) / (jnp.sqrt(square_next / corr_two) + adam_eps)
    values_next = values - update
    return (
        jnp.where(live, values_next, values),
        jnp.where(live, mean_next, mean),
        jnp.where(live, square_next, square),
    )


def make_step(emb_part, weight_part, carry, piece):
    back_part, wgrad = carry
    back = jnp.einsum("mrh,ph->mrp", piece, weight_part, preferred_element_type=jnp.float32)
    back_part = back
    wgrad = wgrad + jnp.einsum("mrp,mrh->ph", emb_part, piece, preferred_element_type=jnp.float32)
    return (back_part, wgrad)


def local(
    embedded,
    resid_grad,
    query_grad,
    query_weight,
    ngram_rows,
    touched_rows,
    row_values,
    row_mean,
    row_square,
):
    micro_count, group_tokens, width_part = embedded.shape
    hidden = query_grad.shape[2]
    tables = lax.axis_size("table")
    table_idx = lax.axis_index("table")
    zero_grad = jnp.zeros((width_part, hidden), jnp.float32)
    wgrad = zero_grad
    backs = []
    for micro in range(micro_count):
        start_back = jnp.zeros((1, group_tokens, width_part), jnp.float32)
        back_one, wgrad = make_step(
            embedded[micro : micro + 1],
            query_weight,
            (start_back, wgrad),
            lax.all_gather(query_grad[micro : micro + 1], "table", axis=1, tiled=True),
        )
        backs.append(back_one)
    back_all = jnp.concatenate(backs, axis=0)
    emb_grad = resid_grad.astype(jnp.float32) + back_all
    weight_grad = lax.psum(wgrad, "dp")
    slice_idx = table_idx * width_part // SW
    ids = lax.dynamic_index_in_dim(ngram_rows, slice_idx, 2, False)
    listed = lax.dynamic_index_in_dim(touched_rows, slice_idx, 1, False)
    entries = listed.shape[1]
    flat_list = listed.reshape(tables * entries)
    onehot = (ids[:, :, None] == flat_list[None, None, :]).astype(jnp.float32)
    buckets = jnp.einsum(
        "mtk,mtp->kp",
        onehot,
        emb_grad,
        precision=lax.Precision.HIGHEST,
        preferred_element_type=jnp.float32,
    )
    buckets = buckets.reshape(tables, entries, width_part)
    arrived = lax.all_to_all(buckets, "table", split_axis=0, concat_axis=0, tiled=True)
    per_slice = tables // SLICES
    local_grad = (
        arrived.reshape(SLICES, per_slice, entries, width_part)
        .transpose(0, 2, 1, 3)
        .reshape(SLICES, entries, per_slice * width_part)
    )
    mine = lax.dynamic_index_in_dim(touched_rows, table_idx, 0, False)
    live = (mine >= 0)[..., None]
    values = row_values[0]
    mean = row_mean[0]
    square = row_square[0]
    grads = lax.psum(local_grad, "dp")
    values_next, mean_next, square_next = adam_rows(grads, values, mean, square, live)
    return (weight_grad, values_next[None], mean_next[None], square_next[None])


def solution(mesh):
    placed = (
        P(None, "dp", "table"),
        P(None, "dp", "table"),
        P(None, ("dp", "table"), None),
        P("table", None),
        P(None, "dp", None),
        P(),
        P("table", None, None, None),
        P("table", None, None, None),
        P("table", None, None, None),
    )
    return jax.shard_map(
        local,
        mesh=mesh,
        in_specs=placed,
        out_specs=(
            P("table", None),
            P("table", None, None, None),
            P("table", None, None, None),
            P("table", None, None, None),
        ),
        check_vma=False,
    )
```

profile of v0, /device:TPU:25, one launch (start us, length us, event | category | flops | bytes accessed | tf_op | source)
XLA Modules:
  0.0 381.5 jit_solution(2230396503521548309)
XLA Ops:
  7.2 0.0 copy-start
  7.2 0.0 all-gather.5.cloned.1.call-start
  7.2 1.9 fusion.37
  9.1 0.0 all-gather.5.cloned.1.call-update
  9.2 0.0 all-gather.3.cloned.1.call-start
  9.2 0.7 all-gather.3.cloned.1.call-update
  9.9 0.9 constant_dynamic-slice_fusion.1
  10.8 0.8 constant_dynamic-slice_fusion
  11.6 0.1 copy.22
  11.7 0.1 eq.19
  11.8 107.7 %all-gather.5.cloned.1.call-done = bf16[1,2048,2048]{2,1,0:T(8,128)(2,1)} async-done(((bf16[1,64,2048]{2,1,0:T(8,128)(2,1)}), bf16[1,2048,2048]{2,1,0:T(8,128)(2,1)}) %all-gather.5.cloned.1.call-update) | async-done | bytes 8388624 | tf_op jit(solution)/shard_map/all_gather | solution.py:61
  119.5 0.0 copy-done
  119.5 6.7 %fusion.15 = f32[1,2048,128]{2,1,0:T(8,128)} fusion(bf16[128,2048]{1,0:T(8,128)(2,1)S(1)} %copy-done, bf16[1,2048,2048]{2,1,0:T(8,128)(2,1)} %all-gather.5.cloned.1.call-done), kind=kOutput, calls=%fused_computation.13 | convolution fusion | flops 1073741824 | bytes 9961472 | tf_op jit(solution)/shard_map/mrh,ph->mrp/dot_general | solution.py:31
  126.2 0.0 copy-start.6
  126.2 0.0 copy-start.1
  126.2 97.1 %all-gather.3.cloned.1.call-done = bf16[1,2048,2048]{2,1,0:T(8,128)(2,1)} async-done(((bf16[1,64,2048]{2,1,0:T(8,128)(2,1)}), bf16[1,2048,2048]{2,1,0:T(8,128)(2,1)}) %all-gather.3.cloned.1.call-update) | async-done | bytes 8388624 | tf_op jit(solution)/shard_map/all_gather | solution.py:61
  223.3 0.0 copy-start.7
  223.3 5.9 %fusion.12 = f32[1,2048,128]{2,1,0:T(8,128)S(1)} fusion(bf16[128,2048]{1,0:T(8,128)(2,1)S(1)} %copy-done, bf16[1,2048,2048]{2,1,0:T(8,128)(2,1)} %all-gather.3.cloned.1.call-done), kind=kOutput, calls=%fused_computation.12 | convolution fusion | flops 1073741824 | bytes 9961472 | tf_op jit(solution)/shard_map/mrh,ph->mrp/dot_general | solution.py:31
  229.1 0.0 copy-done.6
  229.1 0.0 copy-done.7
  229.2 3.1 fusion.24
  232.3 0.7 reshape.46
  233.0 5.2 %all-to-all-start = ((f32[32,12,128]{2,1,0:T(8,128)}), f32[32,12,128]{2,1,0:T(8,128)S(1)}, u32[]{:S(2)}, u32[]{:S(2)}) async-start(f32[32,12,128]{2,1,0:T(8,128)} %reshape.46), calls=%async_computation | async-start | bytes 524288 | tf_op jit(solution)/shard_map/all_to_all | solution.py:81
  238.1 0.2 all-reduce.3.cloned.1.call-start
  238.4 0.0 copy-done.1
  238.4 4.7 %fusion.2 = f32[128,2048]{1,0:T(8,128)S(1)} fusion(bf16[1,2048,2048]{2,1,0:T(8,128)(2,1)} %all-gather.5.cloned.1.call-done, bf16[2,2048,128]{2,1,0:T(8,128)(2,1)S(1)} %copy-done.1), kind=kOutput, calls=%fused_computation.2 | convolution fusion | flops 1073741824 | bytes 9961472 | tf_op jit(solution)/shard_map/mrp,mrh->ph/dot_general | solution.py:33
  243.0 0.0 copy-start.5
  243.1 0.0 copy-start.2
  243.1 0.0 copy-start.3
  243.1 0.0 copy-start.4
  243.1 5.7 %fusion.18 = f32[128,2048]{1,0:T(8,128)} fusion(f32[128,2048]{1,0:T(8,128)S(1)} %fusion.2, bf16[1,2048,2048]{2,1,0:T(8,128)(2,1)} %all-gather.3.cloned.1.call-done, bf16[2,2048,128]{2,1,0:T(8,128)(2,1)S(1)} %copy-done.1), kind=kOutput, calls=%fused_computation.14 | convolution fusion | flops 1074003968 | bytes 11010048 | tf_op jit(solution)/shard_map/mrp,mrh->ph/dot_general | solution.py:33
  248.8 0.0 all-to-all-done
  248.8 0.1 copy.23
  248.9 0.7 reshape.48
  249.6 0.0 all-reduce.3.cloned.1.call-update
  249.6 0.0 copy-done.5
  249.6 0.1 constant_dynamic-slice_fusion.2
  249.7 0.1 copy.25
  249.8 0.1 copy.21
  250.0 120.6 %all-reduce.3.cloned.1.call-done = (f32[128,2048]{1,0:T(8,128)}, f32[4,12,1024]{2,0,1:T(4,128)}) async-done(((f32[128,2048]{1,0:T(8,128)}, f32[4,12,1024]{2,0,1:T(4,128)}), (f32[128,2048]{1,0:T(8,128)}, f32[4,12,1024]{2,0,1:T(4,128)})) %all-reduce.3.cloned.1.call-update) | async-done | bytes 1245200 | tf_op jit(solution)/shard_map/psum | solution.py:66
  370.5 0.0 copy-done.2
  370.5 0.0 copy-done.3
  370.5 0.0 copy-done.4
  370.6 2.1 fusion.33
  372.7 2.3 copy.30
  (2 shorter events, 0.0 us)
Async XLA Ops:
  7.2 112.3 %copy-start = (bf16[128,2048]{1,0:T(8,128)(2,1)S(1)}, bf16[128,2048]{1,0:T(8,128)(2,1)}, u32[]{:S(2)}) copy-start(bf16[128,2048]{1,0:T(8,128)(2,1)} %param.12) | copy-start | bytes 1572868
  7.2 112.3 %all-gather.5.cloned.1.call-start = ((), (), s32[]{:S(2)}) async-start(), calls=%async_computation.2 | async-start | bytes 8650752 | tf_op jit(solution)/shard_map/all_gather | solution.py:61
  9.2 214.1 %all-gather.3.cloned.1.call-start = ((), (), s32[]{:S(2)}) async-start(), calls=%async_computation.1 | async-start | bytes 8650752 | tf_op jit(solution)/shard_map/all_gather | solution.py:61
  126.2 103.0 %copy-start.6 = (bf16[2,2048,128]{2,1,0:T(8,128)(2,1)S(1)}, bf16[2,2048,128]{2,1,0:T(8,128)(2,1)}, u32[]{:S(2)}) copy-start(bf16[2,2048,128]{2,1,0:T(8,128)(2,1)} %param.10) | copy-start | bytes 3145732
  126.2 112.2 %copy-start.1 = (bf16[2,2048,128]{2,1,0:T(8,128)(2,1)S(1)}, bf16[2,2048,128]{2,1,0:T(8,128)(2,1)}, u32[]{:S(2)}) copy-start(bf16[2,2048,128]{2,1,0:T(8,128)(2,1)} %param.9) | copy-start | bytes 3145732
  223.3 5.9 %copy-start.7 = (f32[1,2048,128]{2,1,0:T(8,128)S(1)}, f32[1,2048,128]{2,1,0:T(8,128)}, u32[]{:S(2)}) copy-start(f32[1,2048,128]{2,1,0:T(8,128)} %fusion.15) | copy-start | bytes 3145732
  233.0 15.8 %all-to-all-start = ((f32[32,12,128]{2,1,0:T(8,128)}), f32[32,12,128]{2,1,0:T(8,128)S(1)}, u32[]{:S(2)}, u32[]{:S(2)}) async-start(f32[32,12,128]{2,1,0:T(8,128)} %reshape.46), calls=%async_computation | async-start | bytes 524288 | tf_op jit(solution)/shard_map/all_to_all | solution.py:81
  238.1 132.4 %all-reduce.3.cloned.1.call-start = ((), (), s32[]{:S(2)}) async-start(), calls=%async_computation.3 | async-start | bytes 2490368 | tf_op jit(solution)/shard_map/psum | solution.py:66
  243.0 6.6 %copy-start.5 = (s32[32,4,12]{0,1,2:T(4,128)S(1)}, s32[32,4,12]{0,1,2:T(4,128)}, u32[]{:S(2)}) copy-start(s32[32,4,12]{0,1,2:T(4,128)} %param.14) | copy-start | bytes 18436
  243.1 127.5 %copy-start.2 = (f32[1,4,12,1024]{3,1,2,0:T(4,128)S(1)}, f32[1,4,12,1024]{3,1,2,0:T(4,128)}, u32[]{:S(2)}) copy-start(f32[1,4,12,1024]{3,1,2,0:T(4,128)} %param.17) | copy-start | bytes 589828
  243.1 127.5 %copy-start.3 = (f32[1,4,12,1024]{3,1,2,0:T(4,128)S(1)}, f32[1,4,12,1024]{3,1,2,0:T(4,128)}, u32[]{:S(2)}) copy-start(f32[1,4,12,1024]{3,1,2,0:T(4,128)} %param.16) | copy-start | bytes 589828
  243.1 127.5 %copy-start.4 = (f32[1,4,12,1024]{3,1,2,0:T(4,128)S(1)}, f32[1,4,12,1024]{3,1,2,0:T(4,128)}, u32[]{:S(2)}) copy-start(f32[1,4,12,1024]{3,1,2,0:T(4,128)} %param.15) | copy-start | bytes 589828
Sparse Core Ops, SparseCore 0:
  11.7 107.6 all-gather.4
  122.6 100.5 all-gather.2
  249.8 120.7 all-reduce.2
where the time goes:
time: 382 us
  waiting for transfers between devices  326 us (85%)
  matrix products  26 us (7%)
  between operations  13.9 us (4%)
  local copies, waits for them, and re-layouts  7.9 us (2%)
  starting transfers between devices  5.46 us (1%)
    all_gather x2, waiting for transfers between devices, local(): lax.all_gather(query_grad[micro:micro + 1], 'table', axis=1, tiled=True)  205 us
    psum x1, waiting for transfers between devices, local(): weight_grad = lax.psum(wgrad, 'dp')  121 us
    dot_general x2, matrix products, make_step(): jnp.einsum('mrh,ph->mrp', piece, weight_part, preferred_element_type=jnp....  12.6 us
    dot_general x2, matrix products, make_step(): jnp.einsum('mrp,mrh->ph', emb_part, piece, preferred_element_type=jnp.flo...  10.4 us
  transfers between devices with their start and end apart: 4, of which 3 were waited for; matrix products, arithmetic and copies ran while one was open for 5% of the time, Pallas kernels for 0%

commit v1 on v0

--- a/solution.py
+++ b/solution.py
@@ -63,7 +63,12 @@
         backs.append(back_one)
     back_all = jnp.concatenate(backs, axis=0)
     emb_grad = resid_grad.astype(jnp.float32) + back_all
-    weight_grad = lax.psum(wgrad, "dp")
+    weight_grad = wgrad
+    amount_of = lax.axis_size("dp")
+    for to_i in [k0 for k0 in (1, 2, 4, 8, 16) if k0 < amount_of]:
+        weight_grad = weight_grad + lax.ppermute(
+            weight_grad, "dp", tuple(((w, w ^ to_i) for w in range(amount_of)))
+        )
     slice_idx = table_idx * width_part // SW
     ids = lax.dynamic_index_in_dim(ngram_rows, slice_idx, 2, False)
     listed = lax.dynamic_index_in_dim(touched_rows, slice_idx, 1, False)

time: 382 us -> 459 us (1.20)
  the two profiles are of different devices: /device:TPU:25 before, /device:TPU:1 now
where the time goes in v1:
time: 459 us
  waiting for transfers between devices  388 us (85%)
  matrix products  24.2 us (5%)
  starting transfers between devices  23.7 us (5%)
  between operations  14 us (3%)
  local copies, waits for them, and re-layouts  4.91 us (1%)
    all_gather x2, waiting for transfers between devices, local(): lax.all_gather(query_grad[micro:micro + 1], 'table', axis=1, tiled=True)  210 us
    psum x1, waiting for transfers between devices, local(): grads = lax.psum(local_grad, 'dp')  111 us
    ppermute x4, waiting for transfers between devices, local(): lax.ppermute(weight_grad, 'dp', tuple(((w, w ^ to_i) for w in range(amoun...  58 us
    ppermute x4, starting transfers between devices, local(): lax.ppermute(weight_grad, 'dp', tuple(((w, w ^ to_i) for w in range(amoun...  18.5 us
    dot_general x2, matrix products, make_step(): jnp.einsum('mrh,ph->mrp', piece, weight_part, preferred_element_type=jnp....  11.6 us
    dot_general x2, matrix products, make_step(): jnp.einsum('mrp,mrh->ph', emb_part, piece, preferred_element_type=jnp.flo...  9.5 us
    all_to_all x1, waiting for transfers between devices, local(): lax.all_to_all(buckets, 'table', split_axis=0, concat_axis=0, tiled=True)  9.44 us
  transfers between devices with their start and end apart: 8, of which 7 were waited for; matrix products, arithmetic and copies ran while one was open for 5% of the time, Pallas kernels for 0%

profile of v1, /device:TPU:1, one launch (start us, length us, event | category | flops | bytes accessed | tf_op | source)
XLA Modules:
  0.0 459.0 jit_solution(11360130986125192399)
XLA Ops:
  7.2 0.0 copy-start
  7.2 0.0 copy-start.1
  7.2 0.0 all-gather.5.cloned.1.call-start
  7.2 2.0 fusion.37
  9.2 0.0 all-gather.5.cloned.1.call-update
  9.2 0.0 all-gather.3.cloned.1.call-start
  9.3 0.7 all-gather.3.cloned.1.call-update
  10.0 110.0 %all-gather.5.cloned.1.call-done = bf16[1,2048,2048]{2,1,0:T(8,128)(2,1)} async-done(((bf16[1,64,2048]{2,1,0:T(8,128)(2,1)}), bf16[1,2048,2048]{2,1,0:T(8,128)(2,1)}) %all-gather.5.cloned.1.call-update) | async-done | bytes 8388624 | tf_op jit(solution)/shard_map/all_gather | solution.py:61
  120.0 4.8 %fusion.2 = f32[128,2048]{1,0:T(8,128)S(1)} fusion(bf16[1,2048,2048]{2,1,0:T(8,128)(2,1)} %all-gather.5.cloned.1.call-done, bf16[2,2048,128]{2,1,0:T(8,128)(2,1)} %param.9), kind=kOutput, calls=%fused_computation.2 | convolution fusion | flops 1073741824 | bytes 9961472 | tf_op jit(solution)/shard_map/mrp,mrh->ph/dot_general | solution.py:33
  124.8 0.0 copy-start.4
  124.8 99.5 %all-gather.3.cloned.1.call-done = bf16[1,2048,2048]{2,1,0:T(8,128)(2,1)} async-done(((bf16[1,64,2048]{2,1,0:T(8,128)(2,1)}), bf16[1,2048,2048]{2,1,0:T(8,128)(2,1)}) %all-gather.3.cloned.1.call-update) | async-done | bytes 8388624 | tf_op jit(solution)/shard_map/all_gather | solution.py:61
  224.4 0.0 copy-done.1
  224.4 4.7 %fusion.18 = f32[128,2048]{1,0:T(8,128)S(1)} fusion(f32[128,2048]{1,0:T(8,128)S(1)} %fusion.2, bf16[1,2048,2048]{2,1,0:T(8,128)(2,1)} %all-gather.3.cloned.1.call-done, bf16[2,2048,128]{2,1,0:T(8,128)(2,1)S(1)} %copy-done.1), kind=kOutput, calls=%fused_computation.14 | convolution fusion | flops 1074003968 | bytes 11010048 | tf_op jit(solution)/shard_map/mrp,mrh->ph/dot_general | solution.py:33
  229.0 3.3 collective-permute-start
  232.4 2.3 collective-permute-done
  234.6 0.1 add.44
  234.8 3.1 collective-permute-start.1
  237.9 0.9 constant_dynamic-slice_fusion.1
  238.8 0.0 copy-done.4
  238.8 0.1 copy.22
  238.9 0.1 eq.19
  239.0 22.0 %collective-permute-done.1 = f32[128,2048]{1,0:T(8,128)S(1)} collective-permute-done((f32[128,2048]{1,0:T(8,128)S(1)}, f32[128,2048]{1,0:T(8,128)S(1)}, u32[]{:S(2)}, u32[]{:S(2)}) %collective-permute-start.1) | collective-permute-done | bytes 1048608 | tf_op jit(solution)/shard_map/ppermute | solution.py:69
  261.0 0.1 add.45
  261.2 4.0 collective-permute-start.2
  265.2 5.8 %fusion.15 = f32[1,2048,128]{2,1,0:T(8,128)S(1)} fusion(bf16[128,2048]{1,0:T(8,128)(2,1)S(1)} %copy-done, bf16[1,2048,2048]{2,1,0:T(8,128)(2,1)} %all-gather.5.cloned.1.call-done), kind=kOutput, calls=%fused_computation.13 | convolution fusion | flops 1073741824 | bytes 9961472 | tf_op jit(solution)/shard_map/mrh,ph->mrp/dot_general | solution.py:31
  271.0 0.0 copy-start.5
  271.0 5.8 %fusion.12 = f32[1,2048,128]{2,1,0:T(8,128)S(1)} fusion(bf16[128,2048]{1,0:T(8,128)(2,1)S(1)} %copy-done, bf16[1,2048,2048]{2,1,0:T(8,128)(2,1)} %all-gather.3.cloned.1.call-done), kind=kOutput, calls=%fused_computation.12 | convolution fusion | flops 1073741824 | bytes 9961472 | tf_op jit(solution)/shard_map/mrh,ph->mrp/dot_general | solution.py:31
  276.8 0.0 copy-start.2
  276.9 0.0 copy-start.3
  276.9 33.7 %collective-permute-done.2 = f32[128,2048]{1,0:T(8,128)S(1)} collective-permute-done((f32[128,2048]{1,0:T(8,128)S(1)}, f32[128,2048]{1,0:T(8,128)S(1)}, u32[]{:S(2)}, u32[]{:S(2)}) %collective-permute-start.2) | collective-permute-done | bytes 1048608 | tf_op jit(solution)/shard_map/ppermute | solution.py:69
  310.6 0.1 add.46
  310.7 8.0 %collective-permute-start.3 = (f32[128,2048]{1,0:T(8,128)S(1)}, f32[128,2048]{1,0:T(8,128)S(1)}, u32[]{:S(2)}, u32[]{:S(2)}) collective-permute-start(f32[128,2048]{1,0:T(8,128)S(1)} %add.46), channel_id=1, source_target_pairs={{0,256},{32,288},{64,320},{96,352},{128,384},{160,416},{192,448},{... | collective-permute-start | bytes 3145736 | tf_op jit(solution)/shard_map/ppermute | solution.py:69
  318.7 3.1 fusion.24
  321.8 0.7 reshape.46
  322.6 5.2 %all-to-all-start = ((f32[32,12,128]{2,1,0:T(8,128)}), f32[32,12,128]{2,1,0:T(8,128)S(1)}, u32[]{:S(2)}, u32[]{:S(2)}) async-start(f32[32,12,128]{2,1,0:T(8,128)} %reshape.46), calls=%async_computation | async-start | bytes 524288 | tf_op jit(solution)/shard_map/all_to_all | solution.py:86
  327.7 0.0 all-reduce.2.cloned.1.call-start
  327.8 0.1 constant_dynamic-slice_fusion.2
  327.9 0.1 copy.25
  328.0 9.4 %all-to-all-done = f32[32,12,128]{2,1,0:T(8,128)S(1)} async-done(((f32[32,12,128]{2,1,0:T(8,128)}), f32[32,12,128]{2,1,0:T(8,128)S(1)}, u32[]{:S(2)}, u32[]{:S(2)}) %all-to-all-start) | async-done | bytes 196640 | tf_op jit(solution)/shard_map/all_to_all | solution.py:86
  337.4 0.1 copy.23
  337.5 0.7 reshape.48
  338.2 0.0 all-reduce.2.cloned.1.call-update
  338.3 0.1 copy.21
  338.4 110.8 %all-reduce.2.cloned.1.call-done = f32[4,12,1024]{2,0,1:T(4,128)} async-done(((f32[4,12,1024]{2,0,1:T(4,128)}), f32[4,12,1024]{2,0,1:T(4,128)}) %all-reduce.2.cloned.1.call-update) | async-done | bytes 196624 | tf_op jit(solution)/shard_map/psum | solution.py:98
  449.2 0.0 copy-done.3
  449.2 2.2 fusion.33
  451.4 0.0 collective-permute-done.3
  451.4 1.1 add.47
  (6 shorter events, 0.0 us)
Async XLA Ops:
  7.2 258.0 %copy-start = (bf16[128,2048]{1,0:T(8,128)(2,1)S(1)}, bf16[128,2048]{1,0:T(8,128)(2,1)}, u32[]{:S(2)}) copy-start(bf16[128,2048]{1,0:T(8,128)(2,1)} %param.12) | copy-start | bytes 1572868
  7.2 217.2 %copy-start.1 = (bf16[2,2048,128]{2,1,0:T(8,128)(2,1)S(1)}, bf16[2,2048,128]{2,1,0:T(8,128)(2,1)}, u32[]{:S(2)}) copy-start(bf16[2,2048,128]{2,1,0:T(8,128)(2,1)} %param.9) | copy-start | bytes 3145732
  7.2 112.8 %all-gather.5.cloned.1.call-start = ((), (), s32[]{:S(2)}) async-start(), calls=%async_computation.2 | async-start | bytes 8650752 | tf_op jit(solution)/shard_map/all_gather | solution.py:61
  9.2 215.1 %all-gather.3.cloned.1.call-start = ((), (), s32[]{:S(2)}) async-start(), calls=%async_computation.1 | async-start | bytes 8650752 | tf_op jit(solution)/shard_map/all_gather | solution.py:61
  124.8 114.0 %copy-start.4 = (s32[32,4,12]{0,1,2:T(4,128)S(1)}, s32[32,4,12]{0,1,2:T(4,128)}, u32[]{:S(2)}) copy-start(s32[32,4,12]{0,1,2:T(4,128)} %param.14) | copy-start | bytes 18436
  229.0 5.6 %collective-permute-start = (f32[128,2048]{1,0:T(8,128)S(1)}, f32[128,2048]{1,0:T(8,128)S(1)}, u32[]{:S(2)}, u32[]{:S(2)}) collective-permute-start(f32[128,2048]{1,0:T(8,128)S(1)} %fusion.18), channel_id=1, source_target_pairs={{0,32},{32,0},{64,96},{96,64},{128,160},{160,128},{192,224},{224,1... | collective-permute-start | bytes 3145736 | tf_op jit(solution)/shard_map/ppermute | solution.py:69
  234.8 26.2 %collective-permute-start.1 = (f32[128,2048]{1,0:T(8,128)S(1)}, f32[128,2048]{1,0:T(8,128)S(1)}, u32[]{:S(2)}, u32[]{:S(2)}) collective-permute-start(f32[128,2048]{1,0:T(8,128)S(1)} %add.44), channel_id=1, source_target_pairs={{0,64},{32,96},{64,0},{96,32},{128,192},{160,224},{192,128},{224,1... | collective-permute-start | bytes 3145736 | tf_op jit(solution)/shard_map/ppermute | solution.py:69
  261.2 49.4 %collective-permute-start.2 = (f32[128,2048]{1,0:T(8,128)S(1)}, f32[128,2048]{1,0:T(8,128)S(1)}, u32[]{:S(2)}, u32[]{:S(2)}) collective-permute-start(f32[128,2048]{1,0:T(8,128)S(1)} %add.45), channel_id=1, source_target_pairs={{0,128},{32,160},{64,192},{96,224},{128,0},{160,32},{192,64},{224,... | collective-permute-start | bytes 3145736 | tf_op jit(solution)/shard_map/ppermute | solution.py:69
  271.0 47.8 %copy-start.5 = (bf16[2,2048,128]{2,1,0:T(8,128)(2,1)S(1)}, bf16[2,2048,128]{2,1,0:T(8,128)(2,1)}, u32[]{:S(2)}) copy-start(bf16[2,2048,128]{2,1,0:T(8,128)(2,1)} %param.10) | copy-start | bytes 3145732
  276.8 172.3 %copy-start.2 = (f32[1,4,12,1024]{3,1,2,0:T(4,128)S(1)}, f32[1,4,12,1024]{3,1,2,0:T(4,128)}, u32[]{:S(2)}) copy-start(f32[1,4,12,1024]{3,1,2,0:T(4,128)} %param.17) | copy-start | bytes 589828
  276.9 172.3 %copy-start.3 = (f32[1,4,12,1024]{3,1,2,0:T(4,128)S(1)}, f32[1,4,12,1024]{3,1,2,0:T(4,128)}, u32[]{:S(2)}) copy-start(f32[1,4,12,1024]{3,1,2,0:T(4,128)} %param.16) | copy-start | bytes 589828
  310.7 140.7 %collective-permute-start.3 = (f32[128,2048]{1,0:T(8,128)S(1)}, f32[128,2048]{1,0:T(8,128)S(1)}, u32[]{:S(2)}, u32[]{:S(2)}) collective-permute-start(f32[128,2048]{1,0:T(8,128)S(1)} %add.46), channel_id=1, source_target_pairs={{0,256},{32,288},{64,320},{96,352},{128,384},{160,416},{192,448},{... | collective-permute-start | bytes 3145736 | tf_op jit(solution)/shard_map/ppermute | solution.py:69
  322.6 14.8 %all-to-all-start = ((f32[32,12,128]{2,1,0:T(8,128)}), f32[32,12,128]{2,1,0:T(8,128)S(1)}, u32[]{:S(2)}, u32[]{:S(2)}) async-start(f32[32,12,128]{2,1,0:T(8,128)} %reshape.46), calls=%async_computation | async-start | bytes 524288 | tf_op jit(solution)/shard_map/all_to_all | solution.py:86
  327.7 121.4 %all-reduce.2.cloned.1.call-start = ((), (), s32[]{:S(2)}) async-start(), calls=%async_computation.3 | async-start | bytes 393216 | tf_op jit(solution)/shard_map/psum | solution.py:98
Sparse Core Ops, SparseCore 0:
  11.2 108.7 all-gather.4
  123.7 100.5 all-gather.2
  338.4 110.7 all-reduce.1
